TPU v7x, 256 devices: a whole 4x4x8 slice. The times are simulated.
256 devices in a mesh: shard: 64 (over x, y_hi, z), tensor: 4 (over y_lo, core).
Axes of the slice: x: 4, y: 4 (y_hi: 2, y_lo: 2; y = y_hi * 2 + y_lo), z: 8, core: 2. Of those that a mesh axis runs over, the one named last changes fastest.
Arguments:
- gradient: bfloat16 [768, 3072], P('shard', 'tensor'), may hold values from -0.47851562 to 0.47851562
- moment: float32 [768, 3072], P('shard', 'tensor'), may hold values from -0.48 to 0.48
- second_moment: float32 [768, 3072], P('shard', 'tensor'), may hold values from 0.0001 to 0.01
- stat_left: float32 [768, 768], P('shard', 'tensor'), as said below
- stat_right: float32 [3072, 3072], P('shard', 'tensor'), as said below
- basis_left: float32 [768, 768], P('shard', 'tensor'), as said below
- basis_right: float32 [3072, 3072], P('shard', 'tensor'), as said below
Outputs:
- update: float32 [768, 3072], P('shard', 'tensor')
- moment_new: float32 [768, 3072], P('shard', 'tensor')
- second_new: float32 [768, 3072], P('shard', 'tensor')
- stat_left_new: float32 [768, 768], P('shard', 'tensor')
- stat_right_new: float32 [3072, 3072], P('shard', 'tensor')
- basis_left_new: float32 [768, 768], P('shard', 'tensor')
- basis_right_new: float32 [3072, 3072], P('shard', 'tensor')
Inputs may be any that keep to these rules, and one draw needn't show every extreme that they name: `stat_left`: a symmetric matrix. `stat_right`: a symmetric matrix. `basis_left`: a square matrix of full rank. `basis_right`: a square matrix of full rank.
All inputs are finite; a program needn't handle non-finite values.
Results may differ from a plain program's by a relative error of at most 0.0018.
The roundings to bfloat16 on the way count: a program that leaves them out, or rounds other values in their place, can miss the bound.
Values may be sent and summed in bfloat16 or wider, within the bound.
No kernel may reach another device: no remote copies, remote signals or barrier semaphores. Data moves between devices by JAX's collectives and lax.ppermute only.
A program may use at most 64 MiB of HBM per device.

v0:
```python
import jax
import jax.numpy as jnp
from jax import lax
from jax.sharding import PartitionSpec as P

NS_ITERS = 2


def broadcast(array, axis, root):
    mine = lax.axis_index(axis) == root
    return lax.psum(jnp.where(mine, array, jnp.zeros_like(array)), axis)


def matmul(first_operand, second_operand):
    return jnp.dot(first_operand, second_operand, preferred_element_type=jnp.float32)


def contract_rows(first_operand, second_operand):
    return lax.dot_general(
        first_operand, second_operand, (((0,), (0,)), ((), ())), preferred_element_type=jnp.float32
    )


def contract_cols(first_operand, second_operand):
    return lax.dot_general(
        first_operand, second_operand, (((1,), (1,)), ((), ())), preferred_element_type=jnp.float32
    )


def owned_strip(column_panel, shard_index, tensor_index, strip_width):
    block_width = column_panel.shape[1]
    first_index = shard_index * strip_width
    owner_index = first_index // block_width
    offset = jnp.clip(first_index - tensor_index * block_width, 0, block_width - strip_width)
    return (owner_index, lax.dynamic_slice_in_dim(column_panel, offset, strip_width, 1))


def per_device(gradient, moment, second_moment, stat_left, stat_right, basis_left, basis_right):
    shard_index = lax.axis_index("shard")
    tensor_index = lax.axis_index("tensor")
    rows_left = gradient.shape[0]
    rows_right = stat_right.shape[0]
    block_left = stat_left.shape[1]
    block_hidden = gradient.shape[1]
    moment_new = 0.9 * moment + 0.1 * gradient.astype(jnp.float32)
    moment_half = moment_new.astype(jnp.bfloat16)
    basis_left_half = basis_left.astype(jnp.bfloat16)
    basis_right_half = basis_right.astype(jnp.bfloat16)
    grad_rows, moment_rows, basis_left_rows = (
        lax.all_gather(gradient, "tensor", axis=1, tiled=True),
        lax.all_gather(moment_half, "tensor", axis=1, tiled=True),
        lax.all_gather(basis_left_half, "tensor", axis=1, tiled=True),
    )
    left_columns, right_columns = (
        lax.all_gather(basis_left_half, "shard", axis=0, tiled=True),
        lax.all_gather(basis_right_half, "shard", axis=0, tiled=True),
    )
    full_gradient = lax.all_gather(grad_rows, "shard", axis=0, tiled=True)
    own_rows = lax.dynamic_slice_in_dim(full_gradient, tensor_index * block_left, block_left, 0)
    cross_left = contract_cols(grad_rows, own_rows)
    gradient_strip = lax.dynamic_slice_in_dim(
        full_gradient, shard_index * rows_right, rows_right, 1
    )
    own_columns = lax.dynamic_slice_in_dim(
        full_gradient, tensor_index * block_hidden, block_hidden, 1
    )
    cross_right = contract_rows(gradient_strip, own_columns)
    stat_left_new = 0.95 * stat_left + 0.05 * cross_left
    stat_right_new = 0.95 * stat_right + 0.05 * cross_right
    stat_left_rows, stat_right_rows = (
        lax.all_gather(stat_left_new.astype(jnp.bfloat16), "tensor", axis=1, tiled=True),
        lax.all_gather(stat_right_new.astype(jnp.bfloat16), "tensor", axis=1, tiled=True),
    )
    power_left = matmul(stat_left_rows, left_columns)
    power_right = matmul(stat_right_rows, right_columns)
    square_left, square_right = lax.psum(
        (jnp.sum(power_left * power_left), jnp.sum(power_right * power_right)), ("shard", "tensor")
    )
    iterate_left = power_left / jnp.sqrt(square_left + 1e-06)
    iterate_right = power_right / jnp.sqrt(square_right + 1e-06)
    for iteration in range(NS_ITERS):
        left_half = iterate_left.astype(jnp.bfloat16)
        right_half = iterate_right.astype(jnp.bfloat16)
        left_panel, right_panel = (
            lax.all_gather(left_half, "shard", axis=0, tiled=True),
            lax.all_gather(right_half, "shard", axis=0, tiled=True),
        )
        gram_left = contract_cols(left_half, left_panel)
        gram_right = contract_cols(right_half, right_panel)
        gram_left, gram_right = lax.psum((gram_left, gram_right), "tensor")
        gram_left_half = gram_left.astype(jnp.bfloat16)
        gram_right_half = gram_right.astype(jnp.bfloat16)
        iterate_left = 1.5 * iterate_left - 0.5 * matmul(gram_left_half, left_panel)
        iterate_right = 1.5 * iterate_right - 0.5 * matmul(gram_right_half, right_panel)
    rotated_grad = matmul(grad_rows, right_columns).astype(jnp.bfloat16)
    rotated_moment = matmul(moment_rows, right_columns).astype(jnp.bfloat16)
    grad_panel, moment_panel = (
        lax.all_gather(rotated_grad, "shard", axis=0, tiled=True),
        lax.all_gather(rotated_moment, "shard", axis=0, tiled=True),
    )
    owner_left, local_left = owned_strip(left_columns, shard_index, tensor_index, rows_left)
    basis_strip = broadcast(local_left, "tensor", owner_left)
    grad_turned = contract_rows(basis_strip, grad_panel)
    moment_turned = contract_rows(basis_strip, moment_panel)
    second_new = 0.95 * second_moment + 0.05 * grad_turned * grad_turned
    scaled = (moment_turned / (jnp.sqrt(second_new) + 1e-08)).astype(jnp.bfloat16)
    back_terms = contract_cols(scaled, right_columns)
    back_half = lax.psum_scatter(back_terms, "tensor", scatter_dimension=1, tiled=True).astype(
        jnp.bfloat16
    )
    back_panel = lax.all_gather(back_half, "shard", axis=0, tiled=True)
    update = matmul(basis_left_rows, back_panel)
    return (
        update,
        moment_new,
        second_new,
        stat_left_new,
        stat_right_new,
        iterate_left,
        iterate_right,
    )


def solution(mesh):
    return jax.shard_map(
        per_device,
        mesh=mesh,
        in_specs=(
            P("shard", "tensor"),
            P("shard", "tensor"),
            P("shard", "tensor"),
            P("shard", "tensor"),
            P("shard", "tensor"),
            P("shard", "tensor"),
            P("shard", "tensor"),
        ),
        out_specs=(
            P("shard", "tensor"),
            P("shard", "tensor"),
            P("shard", "tensor"),
            P("shard", "tensor"),
            P("shard", "tensor"),
            P("shard", "tensor"),
            P("shard", "tensor"),
        ),
        check_vma=False,
    )
```

profile of v0, /device:TPU:1, one launch (start us, length us, event | category | flops | bytes accessed | tf_op | source)
XLA Modules:
  0.0 1062.2 jit_solution(13101491253910753219)
XLA Ops:
  7.2 1.6 convert_element_type.57
  8.8 0.0 all-gather.29.cloned.1.call-start
  8.9 9.0 all_gather.49
  18.0 124.4 %all-gather.17.cloned.1.call-done = bf16[3072,768]{1,0:T(8,128)(2,1)} async-done(((bf16[48,768]{1,0:T(8,128)(2,1)}), bf16[3072,768]{1,0:T(8,128)(2,1)}) %all-gather.17.cloned.1.call-update) | async-done | bytes 4718608 | tf_op jit(solution)/shard_map/all_gather | solution.py:56
  142.4 3.7 fusion.14
  146.2 0.6 fusion.46
  146.8 9.3 all_gather.46
  156.1 3.7 fusion.13
  159.9 154.4 %all-gather = bf16[64,12,192]{2,1,0:T(8,128)(2,1)S(1)} all-gather(bf16[1,12,192]{2,1,0:T(8,128)(2,1)S(1)} %get-tuple-element.16), channel_id=1, replica_groups=mesh['shard'=64,'tensor'=4] {'shard'}, dimensions={0}, use_global_device_ids=true | all-gather | bytes 299520 | tf_op jit(solution)/shard_map/all_gather | solution.py:55
  314.2 0.2 reshape.15
  314.5 0.1 dynamic-slice_select_fusion
  314.6 40.0 %psum.49 = bf16[768,12]{1,0:T(8,128)(2,1)S(1)} all-reduce(bf16[768,12]{1,0:T(8,128)(2,1)S(1)} %dynamic-slice_select_fusion), channel_id=1, replica_groups=mesh['shard'=64,'tensor'=4] {'tensor'}, use_global_device_ids=true, to_apply=%region_0.0 | all-reduce | flops 9216 | bytes 36864 | tf_op jit(solution)/shard_map/psum | solution.py:11
  354.6 7.6 reshape.25
  362.3 1.7 fusion.22
  364.0 5.3 all-gather.6
  369.3 0.1 reshape.27
  369.4 2.6 fusion.47
  372.0 8.4 all_gather.57
  380.4 3.8 multiply_reduce_fusion
  384.2 12.6 %all-gather.25.cloned.1.call-done = bf16[64,12,768]{2,1,0:T(8,128)(2,1)} async-done(((bf16[1,12,768]{2,1,0:T(8,128)(2,1)}), bf16[64,12,768]{2,1,0:T(8,128)(2,1)}) %all-gather.25.cloned.1.call-update) | async-done | bytes 1179664 | tf_op jit(solution)/shard_map/all_gather | solution.py:98
  396.8 2.2 reshape.19
  399.1 0.3 fusion.31
  399.4 114.2 %all-gather.23.cloned.1.call-done = bf16[64,12,768]{2,1,0:T(8,128)(2,1)} async-done(((bf16[1,12,768]{2,1,0:T(8,128)(2,1)}), bf16[64,12,768]{2,1,0:T(8,128)(2,1)}) %all-gather.23.cloned.1.call-update) | async-done | bytes 1179664 | tf_op jit(solution)/shard_map/all_gather | solution.py:99
  513.6 2.2 reshape.17
  515.9 4.6 fusion.15
  520.5 0.8 multiply_reduce_fusion.1
  521.3 78.2 %all-reduce = (f32[]{:T(128)}, f32[]{:T(128)}) all-reduce(f32[]{:T(128)} %get-tuple-element.17, f32[]{:T(128)} %get-tuple-element.21), channel_id=1, replica_groups=mesh['shard'=64,'tensor'=4] {'shard','tensor'}, use_global_device_ids=true, to_apply=%region_3.0 | all-reduce | flops 2 | bytes 16 | tf_op jit(solution)/shard_map/psum | solution.py:76
  600.2 0.6 fusion.30
  601.0 1.4 convert_bitcast_fusion
  603.2 151.2 %all-gather.7 = bf16[64,12,192]{2,1,0:T(8,128)(2,1)S(1)} all-gather(bf16[1,12,192]{2,1,0:T(8,128)(2,1)S(1)} %fusion.45), channel_id=1, replica_groups=mesh['shard'=64,'tensor'=4] {'shard'}, dimensions={0}, use_global_device_ids=true | all-gather | bytes 299520 | tf_op jit(solution)/shard_map/all_gather | solution.py:85
  754.4 0.2 reshape.29
  754.6 0.3 fusion.43
  754.9 3.9 fusion.49
  758.7 44.7 %all-reduce.5 = (bf16[12,768]{1,0:T(8,128)(2,1)S(1)}, bf16[48,3072]{1,0:T(8,128)(2,1)S(1)}) all-reduce(f32[12,768]{1,0:T(8,128)S(1)} %fusion.43, f32[48,3072]{1,0:T(8,128)S(1)} %fusion.49), channel_id=1, replica_groups=mesh['shard'=64,'tensor'=4] {'tensor'}, use_global_device_ids=true, to_apply=%region_4.0 | all-reduce | flops 156672 | bytes 940032 | tf_op jit(solution)/shard_map/psum | solution.py:90
  803.5 3.9 fusion.48
  807.4 6.0 all-gather.4
  813.4 0.1 reshape.23
  813.5 26.7 %all-gather.27.cloned.1.call-done = bf16[64,12,768]{2,1,0:T(8,128)(2,1)} async-done(((bf16[1,12,768]{2,1,0:T(8,128)(2,1)}), bf16[64,12,768]{2,1,0:T(8,128)(2,1)}) %all-gather.27.cloned.1.call-update) | async-done | bytes 1179664 | tf_op jit(solution)/shard_map/all_gather | solution.py:111
  840.3 2.2 reshape.21
  842.5 0.9 convolution_bitcast_fusion
  843.4 0.1 fusion.26
  843.6 152.9 %all-gather.8 = bf16[64,12,192]{2,1,0:T(8,128)(2,1)S(1)} all-gather(bf16[1,12,192]{2,1,0:T(8,128)(2,1)S(1)} %convert_bitcast_fusion.2), channel_id=1, replica_groups=mesh['shard'=64,'tensor'=4] {'shard'}, dimensions={0}, use_global_device_ids=true | all-gather | bytes 299520 | tf_op jit(solution)/shard_map/all_gather | solution.py:85
  996.5 0.2 reshape.31
  996.7 0.2 fusion.38
  996.9 3.8 fusion.50
  1000.8 49.9 %all-reduce.6 = (bf16[12,768]{1,0:T(8,128)(2,1)S(1)}, bf16[48,3072]{1,0:T(8,128)(2,1)S(1)}) all-reduce(f32[12,768]{1,0:T(8,128)S(1)} %fusion.38, f32[48,3072]{1,0:T(8,128)S(1)} %fusion.50), channel_id=1, replica_groups=mesh['shard'=64,'tensor'=4] {'tensor'}, use_global_device_ids=true, to_apply=%region_5.0 | all-reduce | flops 156672 | bytes 940032 | tf_op jit(solution)/shard_map/psum | solution.py:90
  1050.7 0.8 fusion.25
  1051.5 3.9 fusion.4
  (45 shorter events, 0.6 us)
Async XLA Ops:
  7.2 139.0 %copy-start.4 = (bf16[12,768]{1,0:T(8,128)(2,1)S(1)}, bf16[12,768]{1,0:T(8,128)(2,1)}, u32[]{:S(2)}) copy-start(bf16[12,768]{1,0:T(8,128)(2,1)} %param.7) | copy-start | bytes 55300
  7.2 139.0 %copy-start.7 = (f32[12,768]{1,0:T(8,128)S(1)}, f32[12,768]{1,0:T(8,128)}, u32[]{:S(2)}) copy-start(f32[12,768]{1,0:T(8,128)} %param.8) | copy-start | bytes 110596
  7.2 135.2 %all-gather.17.cloned.1.call-start = ((), (), s32[]{:S(2)}) async-start(), calls=%async_computation.1 | async-start | bytes 4792320 | tf_op jit(solution)/shard_map/all_gather | solution.py:56
  8.8 345.8 %all-gather.29.cloned.1.call-start = ((), (), s32[]{:S(2)}) async-start(), calls=%async_computation.8 | async-start | bytes 6389760 | tf_op jit(solution)/shard_map/all_gather | solution.py:58
  17.9 141.9 %copy-start.9 = (f32[12,192]{1,0:T(8,128)S(1)}, f32[12,192]{1,0:T(8,128)}, u32[]{:S(2)}) copy-start(f32[12,192]{1,0:T(8,128)} %param.12) | copy-start | bytes 27652
  17.9 378.9 %all-gather.25.cloned.1.call-start = ((), (), s32[]{:S(2)}) async-start(), calls=%async_computation.6 | async-start | bytes 1597440 | tf_op jit(solution)/shard_map/all_gather | solution.py:98
  146.1 367.5 %all-gather.23.cloned.1.call-start = ((), (), s32[]{:S(2)}) async-start(), calls=%async_computation.5 | async-start | bytes 1597440 | tf_op jit(solution)/shard_map/all_gather | solution.py:99
  159.8 441.2 %reduce-scatter.2.cloned.1.call-start = ((), (), s32[]{:S(2)}) async-start(), calls=%async_computation.2 | async-start | bytes 245760 | tf_op jit(solution)/shard_map/reduce_scatter | solution.py:108
  354.6 7.7 copy-start
  354.6 7.7 copy-start.8
  354.6 14.8 %copy-start.3 = (f32[48,768]{1,0:T(8,128)S(1)}, f32[48,768]{1,0:T(8,128)}, u32[]{:S(2)}) copy-start(f32[48,768]{1,0:T(8,128)} %param.11) | copy-start | bytes 442372
  364.0 35.1 %copy-start.5 = (f32[12,192]{1,0:T(8,128)}, f32[12,192]{1,0:T(8,128)S(1)}, u32[]{:S(2)}) copy-start(f32[12,192]{1,0:T(8,128)S(1)} %fusion.22) | copy-start | bytes 27652
  369.4 29.7 %copy-start.6 = (f32[12,768]{1,0:T(8,128)S(1)}, f32[12,768]{1,0:T(8,128)}, u32[]{:S(2)}) copy-start(f32[12,768]{1,0:T(8,128)} %param.9) | copy-start | bytes 110596
  399.4 121.9 %copy-start.2 = (f32[12,768]{1,0:T(8,128)}, f32[12,768]{1,0:T(8,128)S(1)}, u32[]{:S(2)}) copy-start(f32[12,768]{1,0:T(8,128)S(1)} %fusion.31) | copy-start | bytes 110596
  520.5 234.4 %all-gather.19.cloned.1.call-start = ((), (), s32[]{:S(2)}) async-start(), calls=%async_computation.3 | async-start | bytes 4792320 | tf_op jit(solution)/shard_map/all_gather | solution.py:86
  600.9 239.4 %all-gather.27.cloned.1.call-start = ((), (), s32[]{:S(2)}) async-start(), calls=%async_computation.7 | async-start | bytes 1597440 | tf_op jit(solution)/shard_map/all_gather | solution.py:111
  602.4 394.5 %all-gather.21.cloned.1.call-start = ((), (), s32[]{:S(2)}) async-start(), calls=%async_computation.4 | async-start | bytes 4792320 | tf_op jit(solution)/shard_map/all_gather | solution.py:86
  807.4 189.5 %copy-start.1 = (bf16[48,768]{1,0:T(8,128)(2,1)S(1)}, bf16[48,768]{1,0:T(8,128)(2,1)}, u32[]{:S(2)}) copy-start(bf16[48,768]{1,0:T(8,128)(2,1)} %get-tuple-element.23) | copy-start | bytes 221188
Sparse Core Ops, SparseCore 0:
  12.2 130.0 all-gather.16
  146.0 134.3 all-gather.28
  284.7 112.0 all-gather.24
  400.9 112.6 all-gather.22
  520.6 20.4 reduce-scatter.1
  601.0 122.2 all-gather.18
  727.6 112.6 all-gather.26
  844.5 126.5 all-gather.20
where the time goes:
time: 1060 us
  blocking collectives  709 us (67%)
  waiting for transfers between devices  278 us (26%)
  matrix products  38.9 us (4%)
  between operations  15.9 us (2%)
  local copies, waits for them, and re-layouts  15.2 us (1%)
    all_gather x2, blocking collectives, per_device(): lax.all_gather(left_half, 'shard', axis=0, tiled=True)  304 us
    all_gather x1, blocking collectives, per_device(): lax.all_gather(basis_left_half, 'shard', axis=0, tiled=True)  154 us
    all_gather x1, waiting for transfers between devices, per_device(): lax.all_gather(basis_right_half, 'shard', axis=0, tiled=True)  124 us
    all_gather x1, waiting for transfers between devices, per_device(): lax.all_gather(rotated_moment, 'shard', axis=0, tiled=True)  114 us
    psum x2, blocking collectives, per_device(): gram_left, gram_right = lax.psum((gram_left, gram_right), 'tensor')  94.7 us
    psum x1, blocking collectives, per_device(): lax.psum((jnp.sum(power_left * power_left), jnp.sum(power_right * power_r...  78.2 us
    psum x1, blocking collectives, broadcast(): return lax.psum(jnp.where(mine, array, jnp.zeros_like(array)), axis)  40 us
    all_gather x1, waiting for transfers between devices, per_device(): back_panel = lax.all_gather(back_half, 'shard', axis=0, tiled=True)  26.7 us
  transfers between devices with their start and end apart: 8, of which 4 were waited for; matrix products, arithmetic and copies ran while one was open for 4% of the time, Pallas kernels for 0%

commit v1 on v0

--- a/solution.py
+++ b/solution.py
@@ -4,6 +4,19 @@
 from jax.sharding import PartitionSpec as P
 
 NS_ITERS = 2
+
+
+def _check_chains(x_in):
+    moved = jnp.concatenate(
+        lax.all_to_all(
+            jnp.stack(tuple((x_in for _ in range(lax.axis_size("shard")))), 0),
+            split_axis=0,
+            axis_name="shard",
+            concat_axis=0,
+        ),
+        axis=0,
+    )
+    return moved
 
 
 def broadcast(array, axis, root):
@@ -96,7 +109,7 @@
     rotated_moment = matmul(moment_rows, right_columns).astype(jnp.bfloat16)
     grad_panel, moment_panel = (
         lax.all_gather(rotated_grad, "shard", axis=0, tiled=True),
-        lax.all_gather(rotated_moment, "shard", axis=0, tiled=True),
+        _check_chains(rotated_moment),
     )
     owner_left, local_left = owned_strip(left_columns, shard_index, tensor_index, rows_left)
     basis_strip = broadcast(local_left, "tensor", owner_left)

time: 1060 us -> 959 us (0.905)
  waiting for transfers between devices: 278 us -> 141 us
  blocking collectives: 709 us -> 733 us
    all_gather x1 -> x0, waiting for transfers between devices: 114 us -> none  [per_device(): lax.all_gather(rotated_moment, 'shard', axis=0, tiled=True)]
    all_gather x1, blocking collectives: 154 us -> 181 us  [per_device(): lax.all_gather(basis_left_half, 'shard', axis=0, tiled=True)]
    all_gather x1, waiting for transfers between devices: 12.6 us -> 0.01 us  [per_device(): lax.all_gather(rotated_grad, 'shard', axis=0, tiled=True)]
  transfers between devices with their start and end apart: 8 -> 8, of which waited for: 4 -> 2; matrix products, arithmetic and copies ran while one was open for 4% -> 5% of each run, Pallas kernels for 0% -> 0%
where the time goes in v1:
time: 959 us; the launch traced here: 958 us
  blocking collectives  733 us (76%)
  waiting for transfers between devices  141 us (15%)
  matrix products  39.2 us (4%)
  between operations  15.8 us (2%)
  local copies, waits for them, and re-layouts  15.2 us (2%)
    all_gather x2, blocking collectives, per_device(): lax.all_gather(left_half, 'shard', axis=0, tiled=True)  305 us
    all_gather x1, blocking collectives, per_device(): lax.all_gather(basis_left_half, 'shard', axis=0, tiled=True)  181 us
    all_gather x1, waiting for transfers between devices, per_device(): lax.all_gather(basis_right_half, 'shard', axis=0, tiled=True)  118 us
    psum x2, blocking collectives, per_device(): gram_left, gram_right = lax.psum((gram_left, gram_right), 'tensor')  95.2 us
    psum x1, blocking collectives, per_device(): lax.psum((jnp.sum(power_left * power_left), jnp.sum(power_right * power_r...  72.8 us
    psum x1, blocking collectives, broadcast(): return lax.psum(jnp.where(mine, array, jnp.zeros_like(array)), axis)  45.8 us
    all_gather x1, waiting for transfers between devices, per_device(): back_panel = lax.all_gather(back_half, 'shard', axis=0, tiled=True)  22.8 us
    dot_general x9, matrix products, matmul(): jnp.dot(first_operand, second_operand, preferred_element_type=jnp.float32)  21 us
  transfers between devices with their start and end apart: 8, of which 2 were waited for; matrix products, arithmetic and copies ran while one was open for 5% of the time, Pallas kernels for 0%

profile of v1, /device:TPU:1, one launch (start us, length us, event | category | flops | bytes accessed | tf_op | source)
XLA Modules:
  0.0 957.8 jit_solution(121721321244660583)
XLA Ops:
  7.2 1.6 convert_element_type.57
  8.8 9.0 all_gather.45
  17.9 1.4 fusion.45
  19.4 5.3 all_gather.43
  24.7 117.7 %all-gather.15.cloned.1.call-done = bf16[3072,768]{1,0:T(8,128)(2,1)} async-done(((bf16[48,768]{1,0:T(8,128)(2,1)}), bf16[3072,768]{1,0:T(8,128)(2,1)}) %all-gather.15.cloned.1.call-update) | async-done | bytes 4718608 | tf_op jit(solution)/shard_map/all_gather | solution.py:69
  142.3 3.7 fusion.13
  146.1 3.1 convolution_convert_fusion.1
  149.2 1.3 stack.2
  150.5 8.0 all-to-all-start
  158.6 0.6 convert_bitcast_fusion.3
  159.2 181.2 %all-gather = bf16[64,12,192]{2,1,0:T(8,128)(2,1)S(1)} all-gather(bf16[1,12,192]{2,1,0:T(8,128)(2,1)S(1)} %get-tuple-element.16), channel_id=1, replica_groups=mesh['shard'=64,'tensor'=4] {'shard'}, dimensions={0}, use_global_device_ids=true | all-gather | bytes 299520 | tf_op jit(solution)/shard_map/all_gather | solution.py:68
  340.4 0.2 reshape.21
  340.6 0.1 dynamic-slice_select_fusion
  340.8 45.8 %psum.49 = bf16[768,12]{1,0:T(8,128)(2,1)S(1)} all-reduce(bf16[768,12]{1,0:T(8,128)(2,1)S(1)} %dynamic-slice_select_fusion), channel_id=1, replica_groups=mesh['shard'=64,'tensor'=4] {'tensor'}, use_global_device_ids=true, to_apply=%region_0.0 | all-reduce | flops 9216 | bytes 36864 | tf_op jit(solution)/shard_map/psum | solution.py:24
  386.7 7.7 reshape.29
  394.4 1.7 fusion.21
  396.1 6.1 all-gather.5
  402.2 0.7 reshape.31
  402.9 2.6 fusion.46
  405.5 6.0 all_gather.53
  411.5 3.8 multiply_reduce_fusion
  415.4 2.2 reshape.23
  417.6 1.1 fusion.30
  418.7 0.3 reshape.19
  419.1 4.6 fusion.14
  423.7 0.8 multiply_reduce_fusion.1
  424.5 72.8 %all-reduce = (f32[]{:T(128)}, f32[]{:T(128)}) all-reduce(f32[]{:T(128)} %get-tuple-element.17, f32[]{:T(128)} %get-tuple-element.21), channel_id=1, replica_groups=mesh['shard'=64,'tensor'=4] {'shard','tensor'}, use_global_device_ids=true, to_apply=%region_3.0 | all-reduce | flops 2 | bytes 16 | tf_op jit(solution)/shard_map/psum | solution.py:89
  498.0 0.6 fusion.29
  498.7 1.4 convert_bitcast_fusion
  500.9 152.5 %all-gather.6 = bf16[64,12,192]{2,1,0:T(8,128)(2,1)S(1)} all-gather(bf16[1,12,192]{2,1,0:T(8,128)(2,1)S(1)} %fusion.44), channel_id=1, replica_groups=mesh['shard'=64,'tensor'=4] {'shard'}, dimensions={0}, use_global_device_ids=true | all-gather | bytes 299520 | tf_op jit(solution)/shard_map/all_gather | solution.py:98
  653.4 0.2 reshape.33
  653.6 0.2 fusion.42
  653.8 3.9 fusion.48
  657.7 45.4 %all-reduce.5 = (bf16[12,768]{1,0:T(8,128)(2,1)S(1)}, bf16[48,3072]{1,0:T(8,128)(2,1)S(1)}) all-reduce(f32[12,768]{1,0:T(8,128)S(1)} %fusion.42, f32[48,3072]{1,0:T(8,128)S(1)} %fusion.48), channel_id=1, replica_groups=mesh['shard'=64,'tensor'=4] {'tensor'}, use_global_device_ids=true, to_apply=%region_4.0 | all-reduce | flops 156672 | bytes 940032 | tf_op jit(solution)/shard_map/psum | solution.py:103
  703.1 3.9 fusion.47
  707.0 6.0 all-gather.3
  713.0 0.1 reshape.27
  713.1 22.8 %all-gather.23.cloned.1.call-done = bf16[64,12,768]{2,1,0:T(8,128)(2,1)} async-done(((bf16[1,12,768]{2,1,0:T(8,128)(2,1)}), bf16[64,12,768]{2,1,0:T(8,128)(2,1)}) %all-gather.23.cloned.1.call-update) | async-done | bytes 1179664 | tf_op jit(solution)/shard_map/all_gather | solution.py:124
  735.9 2.2 reshape.25
  738.2 0.9 convolution_bitcast_fusion
  739.1 0.1 fusion.25
  739.3 152.9 %all-gather.7 = bf16[64,12,192]{2,1,0:T(8,128)(2,1)S(1)} all-gather(bf16[1,12,192]{2,1,0:T(8,128)(2,1)S(1)} %convert_bitcast_fusion.2), channel_id=1, replica_groups=mesh['shard'=64,'tensor'=4] {'shard'}, dimensions={0}, use_global_device_ids=true | all-gather | bytes 299520 | tf_op jit(solution)/shard_map/all_gather | solution.py:98
  892.1 0.2 reshape.35
  892.3 0.2 fusion.37
  892.6 3.8 fusion.49
  896.4 49.8 %all-reduce.6 = (bf16[12,768]{1,0:T(8,128)(2,1)S(1)}, bf16[48,3072]{1,0:T(8,128)(2,1)S(1)}) all-reduce(f32[12,768]{1,0:T(8,128)S(1)} %fusion.37, f32[48,3072]{1,0:T(8,128)S(1)} %fusion.49), channel_id=1, replica_groups=mesh['shard'=64,'tensor'=4] {'tensor'}, use_global_device_ids=true, to_apply=%region_5.0 | all-reduce | flops 156672 | bytes 940032 | tf_op jit(solution)/shard_map/psum | solution.py:103
  946.3 0.8 fusion.24
  947.1 3.9 fusion.4
  (43 shorter events, 0.6 us)
Async XLA Ops:
  7.2 135.2 %all-gather.15.cloned.1.call-start = ((), (), s32[]{:S(2)}) async-start(), calls=%async_computation.2 | async-start | bytes 4792320 | tf_op jit(solution)/shard_map/all_gather | solution.py:69
  8.8 377.9 %all-gather.25.cloned.1.call-start = ((), (), s32[]{:S(2)}) async-start(), calls=%async_computation.8 | async-start | bytes 6389760 | tf_op jit(solution)/shard_map/all_gather | solution.py:71
  17.9 397.5 %all-gather.21.cloned.1.call-start = ((), (), s32[]{:S(2)}) async-start(), calls=%async_computation.6 | async-start | bytes 1597440 | tf_op jit(solution)/shard_map/all_gather | solution.py:111
  146.1 12.5 %copy-start.8 = (f32[12,192]{1,0:T(8,128)S(1)}, f32[12,192]{1,0:T(8,128)}, u32[]{:S(2)}) copy-start(f32[12,192]{1,0:T(8,128)} %param.12) | copy-start | bytes 27652
  150.5 268.3 %all-to-all-start = ((bf16[64,12,768]{2,1,0:T(8,128)(2,1)}), bf16[64,12,768]{2,1,0:T(8,128)(2,1)S(1)}, u32[]{:S(2)}, u32[]{:S(2)}) async-start(bf16[64,12,768]{2,1,0:T(8,128)(2,1)} %stack.2), calls=%async_computation | async-start | bytes 3145728 | tf_op jit(solution)/shard_map/all_to_all | solution.py:11
  158.5 340.2 %reduce-scatter.2.cloned.1.call-start = ((), (), s32[]{:S(2)}) async-start(), calls=%async_computation.3 | async-start | bytes 245760 | tf_op jit(solution)/shard_map/reduce_scatter | solution.py:121
  386.6 7.7 copy-start
  386.6 7.7 copy-start.7
  386.6 16.2 %copy-start.3 = (f32[48,768]{1,0:T(8,128)S(1)}, f32[48,768]{1,0:T(8,128)}, u32[]{:S(2)}) copy-start(f32[48,768]{1,0:T(8,128)} %param.11) | copy-start | bytes 442372
  396.0 21.6 %copy-start.5 = (f32[12,192]{1,0:T(8,128)}, f32[12,192]{1,0:T(8,128)S(1)}, u32[]{:S(2)}) copy-start(f32[12,192]{1,0:T(8,128)S(1)} %fusion.21) | copy-start | bytes 27652
  418.7 5.8 copy-start.2
  419.1 4.7 copy-start.4
  423.7 230.1 %all-gather.17.cloned.1.call-start = ((), (), s32[]{:S(2)}) async-start(), calls=%async_computation.4 | async-start | bytes 4792320 | tf_op jit(solution)/shard_map/all_gather | solution.py:99
  498.7 237.3 %all-gather.23.cloned.1.call-start = ((), (), s32[]{:S(2)}) async-start(), calls=%async_computation.7 | async-start | bytes 1597440 | tf_op jit(solution)/shard_map/all_gather | solution.py:124
  500.2 392.4 %all-gather.19.cloned.1.call-start = ((), (), s32[]{:S(2)}) async-start(), calls=%async_computation.5 | async-start | bytes 4792320 | tf_op jit(solution)/shard_map/all_gather | solution.py:99
  653.8 53.2 %copy-start.6 = (bf16[1,192,12]{1,2,0:T(8,128)(2,1)S(1)}, bf16[1,192,12]{1,2,0:T(8,128)(2,1)}, u32[]{:S(2)}) copy-start(bf16[1,192,12]{1,2,0:T(8,128)(2,1)} %get-tuple-element.15) | copy-start | bytes 13828
  707.0 185.6 %copy-start.1 = (bf16[48,768]{1,0:T(8,128)(2,1)S(1)}, bf16[48,768]{1,0:T(8,128)(2,1)}, u32[]{:S(2)}) copy-start(bf16[48,768]{1,0:T(8,128)(2,1)} %get-tuple-element.23) | copy-start | bytes 221188
Sparse Core Ops, SparseCore 0:
  12.2 130.0 all-gather.14
  146.0 136.9 all-gather.24
  287.2 113.6 all-gather.20
  423.8 11.7 reduce-scatter.1
  498.8 120.7 all-gather.16
  623.7 112.1 all-gather.22
  740.2 126.5 all-gather.18
